TPU v7x, 256 devices: a whole 4x4x8 slice. The times are simulated.
256 devices in a mesh: mp: 4 (over z_lo, core), fsdp: 16 (over y, x), dp: 4 (over z_hi).
Axes of the slice: x: 4, y: 4, z: 8 (z_hi: 4, z_lo: 2; z = z_hi * 2 + z_lo), core: 2. Of those that a mesh axis runs over, the one named last changes fastest.
Arguments:
- gen_noise: float32 [4, 4096, 128], P('dp', 'fsdp'), may hold values from -6 to 6
- renoise: float32 [4, 4096, 128], P('dp', 'fsdp'), may hold values from -120 to 120
- gen_step: int32 [4], P('dp'), may hold values from 250 to 999
- renoise_step: int32 [4], P('dp'), may hold values from 20 to 979
- text_pooled: bfloat16 [4, 768], P('dp'), may hold values from -6 to 6
- embed: bfloat16 [3, 64, 3072], replicated, may hold values from -0.75 to 0.75
- mod_weight: bfloat16 [3, 1024, 6144], P(None, None, 'fsdp'), may hold values from -0.1875 to 0.1875
- proj_weight: bfloat16 [3, 3072, 3072], P(None, 'fsdp', 'mp'), may hold values from -0.109375 to 0.109375
- unembed: bfloat16 [3, 64, 3072], P(None, None, 'mp'), may hold values from -0.109375 to 0.109375
Outputs:
- gen_grad: float32 [3072, 3072], P('fsdp', 'mp')
- score_gap: float32 [4, 4096, 128], P('dp', 'fsdp')
All inputs are finite; a program needn't handle non-finite values. Where the computation divides by a largest or mean magnitude, that divisor is 1e-20 or more.
Results may differ from a plain program's by a relative error of at most 0.03.
Values may be sent and summed in bfloat16 or wider, within the bound.
A program may use at most 128 MiB of HBM per device.

v0:
```python
import math
import jax
import jax.numpy as jnp
from jax import lax
from jax.sharding import PartitionSpec as P

D = 3072
CH = 64
TEMB = 256
GUIDANCE = 3.5
EPS_NORM = 1e-06
EPS_GAP = 1e-05


def sinusoid(timesteps):
    half_size = TEMB // 2
    frequency = jnp.exp(-math.log(10000.0) * jnp.arange(half_size, dtype=jnp.float32) / half_size)
    angles = timesteps.astype(jnp.float32)[:, None] * frequency[None, :]
    return jnp.concatenate([jnp.cos(angles), jnp.sin(angles)], axis=1)


def condition(timesteps, pooled):
    joined = jnp.concatenate([sinusoid(timesteps), pooled.astype(jnp.float32)], axis=1)
    return jax.nn.silu(joined).astype(jnp.bfloat16)


def normalize(values):
    average = jnp.mean(values, axis=1, keepdims=True)
    centred = values - average
    variance = jnp.mean(centred * centred, axis=1, keepdims=True)
    return centred * lax.rsqrt(variance + EPS_NORM)


def modulate(normed, modulation):
    return (normed * (1.0 + modulation[D:]) + modulation[:D]).astype(jnp.bfloat16)


def unembed_part(residual_sum, out_weight):
    return lax.dot_general(
        residual_sum.astype(jnp.bfloat16),
        out_weight,
        (((1,), (1,)), ((), ())),
        preferred_element_type=jnp.float32,
    )


def row_product(hidden, weight_piece):
    return jnp.dot(hidden, weight_piece, preferred_element_type=jnp.float32)


def body(
    gen_noise, renoise, gen_step, renoise_step, text_pooled, embed, mod_weight, proj_weight, unembed
):
    quarter = proj_weight.shape[2]
    col_start = lax.axis_index("mp") * quarter
    blank_text = jnp.zeros_like(text_pooled)
    noisy_vec = condition(renoise_step, text_pooled)
    local_mod = jnp.concatenate(
        [
            jnp.dot(
                condition(gen_step, text_pooled), mod_weight[0], preferred_element_type=jnp.float32
            ),
            jnp.dot(noisy_vec, mod_weight[1], preferred_element_type=jnp.float32),
            jnp.dot(
                condition(renoise_step, blank_text),
                mod_weight[1],
                preferred_element_type=jnp.float32,
            ),
            jnp.dot(noisy_vec, mod_weight[2], preferred_element_type=jnp.float32),
        ],
        axis=0,
    )
    modulation = lax.all_gather(local_mod, "fsdp", axis=1, tiled=True)
    latent = gen_noise[0].reshape(-1, CH)
    latent_bf = latent.astype(jnp.bfloat16)
    token_rows = latent.shape[0]
    embedded = jnp.dot(latent_bf, embed[0], preferred_element_type=jnp.float32)
    gen_hidden = modulate(normalize(embedded), modulation[0])
    gen_part = row_product(gen_hidden, lax.all_gather(proj_weight[0], "fsdp", axis=0, tiled=True))
    gen_cols = lax.dynamic_slice_in_dim(embedded, col_start, quarter, 1)
    clean_part = unembed_part(gen_cols + gen_part, unembed[0]).reshape(-1, 2 * CH)
    clean_lat = lax.psum(clean_part, "mp")
    noise_level = renoise_step[0].astype(jnp.float32) / 1000.0
    noisy_lat = (1.0 - noise_level) * clean_lat + noise_level * renoise[0]
    noisy_bf = noisy_lat.reshape(-1, CH).astype(jnp.bfloat16)
    teacher_in = jnp.dot(noisy_bf, embed[1], preferred_element_type=jnp.float32)
    teacher_norm = normalize(teacher_in)
    cond_hidden = modulate(teacher_norm, modulation[1])
    blank_hidden = modulate(teacher_norm, modulation[2])
    fake_in = jnp.dot(noisy_bf, embed[2], preferred_element_type=jnp.float32)
    fake_hidden = modulate(normalize(fake_in), modulation[3])
    pieces = (
        lax.all_gather(proj_weight[1], "fsdp", axis=0, tiled=True),
        lax.all_gather(proj_weight[2], "fsdp", axis=0, tiled=True),
    )
    cond_part = row_product(cond_hidden, pieces[0])
    blank_part = row_product(blank_hidden, pieces[0])
    fake_part = row_product(fake_hidden, pieces[1])
    teacher_cols = lax.dynamic_slice_in_dim(teacher_in, col_start, quarter, 1)
    fake_cols = lax.dynamic_slice_in_dim(fake_in, col_start, quarter, 1)
    cond_out, blank_out, fake_out = (
        lax.psum(
            unembed_part(teacher_cols + cond_part, unembed[1])
            .reshape(-1, 2 * CH)
            .astype(jnp.bfloat16),
            "mp",
        ).astype(jnp.float32),
        lax.psum(
            unembed_part(teacher_cols + blank_part, unembed[1])
            .reshape(-1, 2 * CH)
            .astype(jnp.bfloat16),
            "mp",
        ).astype(jnp.float32),
        lax.psum(
            unembed_part(fake_cols + fake_part, unembed[2])
            .reshape(-1, 2 * CH)
            .astype(jnp.bfloat16),
            "mp",
        ).astype(jnp.float32),
    )
    real_pred = noisy_lat - noise_level * (blank_out + GUIDANCE * (cond_out - blank_out))
    fake_pred = noisy_lat - noise_level * fake_out
    seq_len = token_rows * lax.axis_size("fsdp")
    gap_total = lax.psum(jnp.sum(jnp.abs(clean_lat - real_pred)), "fsdp")
    gap_scale = gap_total / (seq_len * CH) + EPS_GAP
    score_gap = (fake_pred - real_pred) / gap_scale
    all_tokens = seq_len * lax.axis_size("dp")
    cotangent = (score_gap / math.sqrt(all_tokens)).astype(jnp.bfloat16).reshape(-1, CH)
    upstream = jnp.dot(cotangent, unembed[0], preferred_element_type=jnp.float32).astype(
        jnp.bfloat16
    )
    row_terms = lax.psum_scatter(
        lax.dot_general(
            gen_hidden, upstream, (((0,), (0,)), ((), ())), preferred_element_type=jnp.float32
        ).astype(jnp.bfloat16),
        "fsdp",
        scatter_dimension=0,
        tiled=True,
    )
    gen_grad = lax.psum(row_terms, "dp").astype(jnp.float32)
    return (gen_grad, score_gap[None])


def solution(mesh):
    return jax.shard_map(
        body,
        mesh=mesh,
        in_specs=(
            P("dp", "fsdp", None),
            P("dp", "fsdp", None),
            P("dp"),
            P("dp"),
            P("dp", None),
            P(),
            P(None, None, "fsdp"),
            P(None, "fsdp", "mp"),
            P(None, None, "mp"),
        ),
        out_specs=(P("fsdp", "mp"), P("dp", "fsdp", None)),
        check_vma=False,
    )
```

profile of v0, /device:TPU:2, one launch (start us, length us, event | category | flops | bytes accessed | tf_op | source)
XLA Modules:
  0.0 498.5 jit_solution(18427168380381059458)
XLA Ops:
  7.2 0.0 all-gather.7.cloned.1.call-start
  7.2 2.1 fusion.104
  9.3 0.0 all-gather.7.cloned.1.call-update
  9.3 0.0 all-reduce.5.cloned.1.call-start
  9.4 0.9 convert_element_type.109
  10.3 0.1 convert_element_type.110
  11.7 0.1 fusion.100
  11.8 0.7 convert_reduce_fusion
  12.6 1.3 fusion.49
  13.9 1.3 fusion.53
  15.2 1.3 fusion.51
  16.6 1.3 fusion.55
  17.9 0.1 pad_maximum_fusion
  18.0 23.6 %all_gather.12 = f32[4,6144]{1,0:T(4,128)S(1)} all-gather(f32[4,384]{1,0:T(4,128)S(1)} %pad_maximum_fusion), channel_id=1, replica_groups=mesh['mp'=4,'fsdp'=16,'dp'=4] {'fsdp'}, dimensions={1}, use_global_device_ids=true | all-gather | bytes 104448 | tf_op jit(solution)/shard_map/all_gather | solution.py:73
  41.7 2.1 fusion.105
  43.8 2.6 copy-done
  46.4 0.8 multiply_reduce_fusion.2
  47.2 0.1 slice_add_fusion.1
  47.3 25.2 %all-gather.7.cloned.1.call-done = bf16[1,3072,768]{2,1,0:T(8,128)(2,1)} async-done(((bf16[1,192,768]{2,1,0:T(8,128)(2,1)}), bf16[1,3072,768]{2,1,0:T(8,128)(2,1)}) %all-gather.7.cloned.1.call-update) | async-done | bytes 4718608 | tf_op jit(solution)/shard_map/all_gather | solution.py:79
  72.5 0.0 copy-done.6
  72.5 7.9 %fusion.38 = f32[512,64]{1,0:T(8,128)S(1)} fusion(f32[512,3072]{1,0:T(8,128)} %copy-done, s32[]{:T(128)S(6)} %select_n.2, bf16[1,3072,768]{2,1,0:T(8,128)(2,1)} %all-gather.7.cloned.1.call-done, bf16[3,64,768]{2,1,0:T(8,128)(2,1)S(1)} %copy-done.6, f32[3072]{0:T(1024)S(1)} %bitcast.103, f32[3072]{0:T(1024)S(1)} %bitcast.105, f32[512]{0:T(512)S(1)} %add_rsqrt_fusion.2, ...), kind=kOutput, calls=%fused_computation.36 | convolution fusion | flops 2474901504 | bytes 12840964 | tf_op jit(solution)/shard_map/dot_general | solution.py:39
  80.3 0.8 reshape.200
  81.1 0.0 all-reduce.5.cloned.1.call-update
  81.1 0.0 all-gather.9.cloned.1.call-start
  81.2 0.7 all-gather.9.cloned.1.call-update
  81.8 0.0 all-gather.11.cloned.1.call-start
  81.9 0.5 all-gather.11.cloned.1.call-update
  82.4 0.2 all-reduce.9.cloned.1.call-start
  82.7 38.7 %all-reduce.5.cloned.1.call-done = f32[256,128]{1,0:T(8,128)} async-done(((f32[256,128]{1,0:T(8,128)}), f32[256,128]{1,0:T(8,128)}) %all-reduce.5.cloned.1.call-update) | async-done | bytes 131088 | tf_op jit(solution)/shard_map/psum | solution.py:82
  121.3 0.0 copy-done.4
  121.4 0.9 fusion.85
  122.3 0.1 convert_element_type.120
  122.4 0.0 copy-done.3
  122.4 1.0 fusion.106
  123.4 2.7 copy-done.2
  126.1 0.8 multiply_reduce_fusion.1
  126.9 56.7 %all-gather.9.cloned.1.call-done = bf16[1,3072,768]{2,1,0:T(8,128)(2,1)} async-done(((bf16[1,192,768]{2,1,0:T(8,128)(2,1)}), bf16[1,3072,768]{2,1,0:T(8,128)(2,1)}) %all-gather.9.cloned.1.call-update) | async-done | bytes 4718608 | tf_op jit(solution)/shard_map/all_gather | solution.py:94
  183.6 7.9 %fusion.46 = bf16[512,64]{0,1:T(8,128)(2,1)S(1)} fusion(f32[512,3072]{1,0:T(8,128)} %copy-done.2, s32[]{:T(128)S(6)} %select_n.2, bf16[1,3072,768]{2,1,0:T(8,128)(2,1)} %all-gather.9.cloned.1.call-done, f32[3072]{0:T(1024)S(1)} %bitcast.111, f32[3072]{0:T(1024)S(1)} %bitcast.112, f32[512]{0:T(512)S(1)} %add_rsqrt_fusion.1, ...), kind=kOutput, calls=%fused_computation.39 | convolution fusion | flops 2474934272 | bytes 12775428 | tf_op jit(solution)/shard_map/dot_general | solution.py:39
  191.5 0.1 copy.12
  191.6 0.8 convert_element_type.124
  192.4 1.0 fusion.107
  193.4 2.7 copy-done.1
  196.1 0.8 multiply_reduce_fusion
  196.8 48.7 %all-gather.11.cloned.1.call-done = bf16[1,3072,768]{2,1,0:T(8,128)(2,1)} async-done(((bf16[1,192,768]{2,1,0:T(8,128)(2,1)}), bf16[1,3072,768]{2,1,0:T(8,128)(2,1)}) %all-gather.11.cloned.1.call-update) | async-done | bytes 4718608 | tf_op jit(solution)/shard_map/all_gather | solution.py:93
  245.5 7.9 %fusion.40 = bf16[512,64]{0,1:T(8,128)(2,1)S(1)} fusion(f32[512,3072]{1,0:T(8,128)} %copy-done.1, s32[]{:T(128)S(6)} %select_n.2, bf16[1,3072,768]{2,1,0:T(8,128)(2,1)} %all-gather.11.cloned.1.call-done, f32[3072]{0:T(1024)S(1)} %bitcast.109, f32[3072]{0:T(1024)S(1)} %bitcast.110, f32[512]{0:T(512)S(1)} %add_rsqrt_fusion, ...), kind=kOutput, calls=%fused_computation.37 | convolution fusion | flops 2474934272 | bytes 12775428 | tf_op jit(solution)/shard_map/dot_general | solution.py:39
  253.4 0.1 copy.14
  253.5 0.8 convert_element_type.134
  254.3 7.9 %fusion.43 = bf16[512,64]{0,1:T(8,128)(2,1)S(1)} fusion(f32[512,3072]{1,0:T(8,128)} %copy-done.1, s32[]{:T(128)S(6)} %select_n.2, bf16[1,3072,768]{2,1,0:T(8,128)(2,1)} %all-gather.11.cloned.1.call-done, f32[3072]{0:T(1024)S(1)} %bitcast.108, f32[3072]{0:T(1024)S(1)} %bitcast.107, f32[512]{0:T(512)S(1)} %add_rsqrt_fusion, ...), kind=kOutput, calls=%fused_computation.38 | convolution fusion | flops 2474934272 | bytes 12775428 | tf_op jit(solution)/shard_map/dot_general | solution.py:39
  262.2 0.1 copy.13
  262.4 0.8 convert_element_type.129
  263.1 0.0 all-reduce.9.cloned.1.call-update
  263.1 0.0 reduce-scatter.2.cloned.1.call-start
  263.2 40.5 %all-reduce.9.cloned.1.call-done = (bf16[256,128]{1,0:T(8,128)(2,1)}, bf16[256,128]{1,0:T(8,128)(2,1)}, bf16[256,128]{1,0:T(8,128)(2,1)}) async-done(((bf16[256,128]{1,0:T(8,128)(2,1)}, bf16[256,128]{1,0:T(8,128)(2,1)}, bf16[256,128]{1,0:T(8,128)(2,1)}), (bf16[256,128]{1,0:T(8,128)(2,1)}, bf16[256,128]{1,0:T(8,128)(2,1)}, bf16[256,128]{1,0:T(8,128)(2,1)})) %all-reduce.9.cloned.1.call-update) | async-done | bytes 196624 | tf_op jit(solution)/shard_map/psum | solution.py:114
  303.7 1.5 abs_reduce_fusion
  305.2 37.2 %psum.46 = f32[]{:T(128)} all-reduce(f32[]{:T(128)} %abs_reduce_fusion), channel_id=1, replica_groups=mesh['mp'=4,'fsdp'=16,'dp'=4] {'fsdp'}, use_global_device_ids=true, to_apply=%region_11.12 | all-reduce | flops 1 | bytes 8 | tf_op jit(solution)/shard_map/psum | solution.py:124
  343.1 1.6 multiply_convert_fusion
  344.7 0.1 reshape.201
  344.8 8.2 %convolution_convert_fusion = bf16[3072,768]{1,0:T(8,128)(2,1)} fusion(bf16[512,64]{1,0:T(8,128)(2,1)S(1)} %reshape.201, bf16[3,64,768]{2,1,0:T(8,128)(2,1)S(1)} %copy-done.6, f32[512,3072]{1,0:T(8,128)} %copy-done, f32[3072]{0:T(1024)S(1)} %bitcast.104, f32[3072]{0:T(1024)S(1)} %bitcast.106, f32[512]{0:T(512)S(1)} %add_rsqrt_fusion.2, ...), kind=kOutput, calls=%fused_computation.7 | convolution fusion | flops 2476867584 | bytes 11268096 | tf_op jit(solution)/shard_map/dot_general | solution.py:133
  353.0 0.0 reduce-scatter.2.cloned.1.call-update
  353.0 0.0 all-reduce.7.cloned.1.call-start
  353.1 82.9 %reduce-scatter.2.cloned.1.call-done = bf16[192,768]{1,0:T(8,128)(2,1)} async-done(((bf16[3072,768]{1,0:T(8,128)(2,1)}), bf16[192,768]{1,0:T(8,128)(2,1)}) %reduce-scatter.2.cloned.1.call-update) | async-done | bytes 294928 | tf_op jit(solution)/shard_map/reduce_scatter | solution.py:132
  436.0 0.0 all-reduce.7.cloned.1.call-update
  436.0 53.8 %all-reduce.7.cloned.1.call-done = bf16[192,768]{1,0:T(8,128)(2,1)} async-done(((bf16[192,768]{1,0:T(8,128)(2,1)}), bf16[192,768]{1,0:T(8,128)(2,1)}) %all-reduce.7.cloned.1.call-update) | async-done | bytes 294928 | tf_op jit(solution)/shard_map/psum | solution.py:140
  489.8 1.8 convert_element_type.139
  (20 shorter events, 0.1 us)
Async XLA Ops:
  7.2 65.3 %all-gather.7.cloned.1.call-start = ((), (), s32[]{:S(2)}) async-start(), calls=%async_computation.4 | async-start | bytes 5013504 | tf_op jit(solution)/shard_map/all_gather | solution.py:79
  9.3 112.0 %all-reduce.5.cloned.1.call-start = ((), (), s32[]{:S(2)}) async-start(), calls=%async_computation.1 | async-start | bytes 262144 | tf_op jit(solution)/shard_map/psum | solution.py:82
  41.7 30.8 %copy-start.6 = (bf16[3,64,768]{2,1,0:T(8,128)(2,1)S(1)}, bf16[3,64,768]{2,1,0:T(8,128)(2,1)}, u32[]{:S(2)}) copy-start(bf16[3,64,768]{2,1,0:T(8,128)(2,1)} %param.17) | copy-start | bytes 884740
  43.7 2.7 copy-start
  72.5 48.9 %copy-start.4 = (f32[1,256,128]{2,1,0:T(8,128)S(1)}, f32[1,256,128]{2,1,0:T(8,128)}, u32[]{:S(2)}) copy-start(f32[1,256,128]{2,1,0:T(8,128)} %param.10) | copy-start | bytes 393220
  72.5 49.9 %copy-start.3 = (bf16[3,64,3072]{2,1,0:T(8,128)(2,1)S(1)}, bf16[3,64,3072]{2,1,0:T(8,128)(2,1)}, u32[]{:S(2)}) copy-start(bf16[3,64,3072]{2,1,0:T(8,128)(2,1)} %param.14) | copy-start | bytes 3538948
  81.1 102.4 %all-gather.9.cloned.1.call-start = ((), (), s32[]{:S(2)}) async-start(), calls=%async_computation.5 | async-start | bytes 5013504 | tf_op jit(solution)/shard_map/all_gather | solution.py:94
  81.8 163.7 %all-gather.11.cloned.1.call-start = ((), (), s32[]{:S(2)}) async-start(), calls=%async_computation.6 | async-start | bytes 5013504 | tf_op jit(solution)/shard_map/all_gather | solution.py:93
  82.4 221.2 %all-reduce.9.cloned.1.call-start = ((), (), s32[]{:S(2)}) async-start(), calls=%async_computation.7 | async-start | bytes 393216 | tf_op jit(solution)/shard_map/psum | solution.py:114
  123.4 2.7 copy-start.2
  193.4 2.7 copy-start.1
  254.3 49.4 %copy-start.5 = (f32[256,128]{1,0:T(8,128)S(1)}, f32[256,128]{1,0:T(8,128)}, u32[]{:S(2)}) copy-start(f32[256,128]{1,0:T(8,128)} %all-reduce.5.cloned.1.call-done) | copy-start | bytes 393220
  263.1 172.8 %reduce-scatter.2.cloned.1.call-start = ((), (), s32[]{:S(2)}) async-start(), calls=%async_computation.2 | async-start | bytes 5013504 | tf_op jit(solution)/shard_map/reduce_scatter | solution.py:132
  353.0 136.8 %all-reduce.7.cloned.1.call-start = ((), (), s32[]{:S(2)}) async-start(), calls=%async_computation.3 | async-start | bytes 589824 | tf_op jit(solution)/shard_map/psum | solution.py:140
Sparse Core Ops, SparseCore 0:
  10.4 61.9 all-gather.6
  81.2 40.0 all-reduce.4
  124.1 59.4 all-gather.8
  186.7 58.7 all-gather.10
  263.3 40.3 all-reduce.8
  353.2 82.7 reduce-scatter.1
  438.6 51.1 all-reduce.6
where the time goes:
time: 499 us; the launch traced here: 498 us
  waiting for transfers between devices  348 us (70%)
  blocking collectives  60.9 us (12%)
  matrix products  49.3 us (10%)
  between operations  16.3 us (3%)
  local copies, waits for them, and re-layouts  13.7 us (3%)
  other arithmetic  10.1 us (2%)
    reduce_scatter x1, waiting for transfers between devices, body(): lax.psum_scatter(lax.dot_general(gen_hidden, upstream, (((0,), (0,)), (()...  82.9 us
    all_gather x1, waiting for transfers between devices, body(): lax.all_gather(proj_weight[2], 'fsdp', axis=0, tiled=True)  56.7 us
    psum x1, waiting for transfers between devices, body(): gen_grad = lax.psum(row_terms, 'dp').astype(jnp.float32)  53.8 us
    all_gather x1, waiting for transfers between devices, body(): lax.all_gather(proj_weight[1], 'fsdp', axis=0, tiled=True)  48.7 us
    psum x1, waiting for transfers between devices, body(): lax.psum(unembed_part(fake_cols + fake_part, unembed[2]).reshape(-1, 2 *...  40.5 us
    psum x1, waiting for transfers between devices, body(): clean_lat = lax.psum(clean_part, 'mp')  38.7 us
    psum x1, blocking collectives, body(): gap_total = lax.psum(jnp.sum(jnp.abs(clean_lat - real_pred)), 'fsdp')  37.2 us
    dot_general x4, matrix products, unembed_part(): lax.dot_general(residual_sum.astype(jnp.bfloat16), out_weight, (((1,), (1...  31.6 us
  transfers between devices with their start and end apart: 7, of which 7 were waited for; matrix products, arithmetic and copies ran while one was open for 5% of the time, Pallas kernels for 0%

commit v1 on v0

--- a/solution.py
+++ b/solution.py
@@ -10,6 +10,11 @@
 GUIDANCE = 3.5
 EPS_NORM = 1e-06
 EPS_GAP = 1e-05
+
+
+def tiled_gather(array, axis, dim):
+    copies = jnp.concatenate([array] * lax.axis_size(axis), axis=dim)
+    return lax.all_to_all(copies, axis, dim, dim, tiled=True)
 
 
 def sinusoid(timesteps):
@@ -90,7 +95,7 @@
     fake_in = jnp.dot(noisy_bf, embed[2], preferred_element_type=jnp.float32)
     fake_hidden = modulate(normalize(fake_in), modulation[3])
     pieces = (
-        lax.all_gather(proj_weight[1], "fsdp", axis=0, tiled=True),
+        tiled_gather(proj_weight[1], "fsdp", 0),
         lax.all_gather(proj_weight[2], "fsdp", axis=0, tiled=True),
     )
     cond_part = row_product(cond_hidden, pieces[0])

time: 499 us -> 465 us (0.932)
  waiting for transfers between devices: 348 us -> 306 us
  starting transfers between devices: 0.46 us -> 6.27 us
    all_gather x1 -> x0, waiting for transfers between devices: 48.7 us -> none  [body(): lax.all_gather(proj_weight[1], 'fsdp', axis=0, tiled=True)]
    all_gather x1, waiting for transfers between devices: 56.7 us -> 70.8 us  [body(): lax.all_gather(proj_weight[2], 'fsdp', axis=0, tiled=True)]
    psum x1, waiting for transfers between devices: 38.7 us -> 31.3 us  [body(): clean_lat = lax.psum(clean_part, 'mp')]
    all_to_all x0 -> x1, starting transfers between devices: none -> 5.85 us  [tiled_gather(): return lax.all_to_all(copies, axis, dim, dim, tiled=True)]
    unnamed x14 -> x33, local copies, waits for them, and re-layouts: 7.98 us -> 10.4 us
  transfers between devices with their start and end apart: 7 -> 7, of which waited for: 7 -> 6; matrix products, arithmetic and copies ran while one was open for 5% -> 5% of each run, Pallas kernels for 0% -> 0%
where the time goes in v1:
time: 465 us; the launch traced here: 464 us
  waiting for transfers between devices  306 us (66%)
  blocking collectives  60.9 us (13%)
  matrix products  48.3 us (10%)
  between operations  16.5 us (4%)
  local copies, waits for them, and re-layouts  16.1 us (3%)
  other arithmetic  10.1 us (2%)
  starting transfers between devices  6.27 us (1%)
    reduce_scatter x1, waiting for transfers between devices, body(): lax.psum_scatter(lax.dot_general(gen_hidden, upstream, (((0,), (0,)), (()...  82.7 us
    all_gather x1, waiting for transfers between devices, body(): lax.all_gather(proj_weight[2], 'fsdp', axis=0, tiled=True)  70.8 us
    psum x1, waiting for transfers between devices, body(): gen_grad = lax.psum(row_terms, 'dp').astype(jnp.float32)  53.7 us
    psum x1, waiting for transfers between devices, body(): lax.psum(unembed_part(fake_cols + fake_part, unembed[2]).reshape(-1, 2 *...  40.5 us
    psum x1, blocking collectives, body(): gap_total = lax.psum(jnp.sum(jnp.abs(clean_lat - real_pred)), 'fsdp')  37.2 us
    dot_general x4, matrix products, unembed_part(): lax.dot_general(residual_sum.astype(jnp.bfloat16), out_weight, (((1,), (1...  31.7 us
    psum x1, waiting for transfers between devices, body(): clean_lat = lax.psum(clean_part, 'mp')  31.3 us
    all_gather x1, waiting for transfers between devices, body(): lax.all_gather(proj_weight[0], 'fsdp', axis=0, tiled=True)  26.3 us
  transfers between devices with their start and end apart: 7, of which 6 were waited for; matrix products, arithmetic and copies ran while one was open for 5% of the time, Pallas kernels for 0%

profile of v1, /device:TPU:2, one launch (start us, length us, event | category | flops | bytes accessed | tf_op | source)
XLA Modules:
  0.0 464.2 jit_solution(14477814216234139560)
XLA Ops:
  7.2 0.0 copy-start.5
  7.2 0.0 all-gather.5.cloned.1.call-start
  7.2 2.0 fusion.90
  9.2 0.0 all-gather.5.cloned.1.call-update
  9.2 0.0 all-reduce.5.cloned.1.call-start
  9.3 0.9 convert_element_type.109
  10.2 0.1 convert_element_type.110
  11.7 0.1 fusion.86
  11.7 0.7 convert_reduce_fusion
  12.5 1.3 fusion.35
  13.8 1.3 fusion.39
  15.2 1.3 fusion.37
  16.5 1.3 fusion.41
  17.9 0.1 pad_maximum_fusion
  17.9 23.7 %all_gather.9 = f32[4,6144]{1,0:T(4,128)S(1)} all-gather(f32[4,384]{1,0:T(4,128)S(1)} %pad_maximum_fusion), channel_id=1, replica_groups=mesh['mp'=4,'fsdp'=16,'dp'=4] {'fsdp'}, dimensions={1}, use_global_device_ids=true | all-gather | bytes 104448 | tf_op jit(solution)/shard_map/all_gather | solution.py:78
  41.6 0.0 copy-done.5
  41.6 1.0 fusion.91
  42.7 0.0 copy-start.8
  42.7 2.6 copy-done
  45.3 0.8 multiply_reduce_fusion.2
  46.1 0.1 slice_add_fusion.1
  46.2 26.3 %all-gather.5.cloned.1.call-done = bf16[1,3072,768]{2,1,0:T(8,128)(2,1)} async-done(((bf16[1,192,768]{2,1,0:T(8,128)(2,1)}), bf16[1,3072,768]{2,1,0:T(8,128)(2,1)}) %all-gather.5.cloned.1.call-update) | async-done | bytes 4718608 | tf_op jit(solution)/shard_map/all_gather | solution.py:84
  72.5 7.8 %fusion.28 = f32[512,64]{1,0:T(8,128)S(1)} fusion(f32[512,3072]{1,0:T(8,128)} %copy-done, s32[]{:T(128)S(6)} %select_n.2, bf16[1,3072,768]{2,1,0:T(8,128)(2,1)} %all-gather.5.cloned.1.call-done, bf16[3,64,768]{2,1,0:T(8,128)(2,1)S(1)} %copy-done.8, f32[3072]{0:T(1024)S(1)} %bitcast.108, f32[3072]{0:T(1024)S(1)} %bitcast.110, f32[512]{0:T(512)S(1)} %add_rsqrt_fusion.2, ...), kind=kOutput, calls=%fused_computation.34 | convolution fusion | flops 2474901504 | bytes 12840964 | tf_op jit(solution)/shard_map/dot_general | solution.py:44
  80.3 0.8 reshape.202
  81.1 0.0 all-reduce.5.cloned.1.call-update
  81.1 0.0 all-gather.7.cloned.1.call-start
  81.2 0.7 all-gather.7.cloned.1.call-update
  82.4 2.1 copy-done.4
  84.5 5.9 %all-to-all-start = ((bf16[16,192,768]{2,1,0:T(8,128)(2,1)}), bf16[16,192,768]{2,1,0:T(8,128)(2,1)}, u32[]{:S(2)}, u32[]{:S(2)}) async-start(bf16[16,192,768]{2,1,0:T(8,128)(2,1)} %bitcast.106), calls=%async_computation | async-start | bytes 9437184 | tf_op jit(solution)/shard_map/all_to_all | solution.py:17
  90.4 0.2 all-reduce.9.cloned.1.call-start
  90.6 31.3 %all-reduce.5.cloned.1.call-done = f32[256,128]{1,0:T(8,128)} async-done(((f32[256,128]{1,0:T(8,128)}), f32[256,128]{1,0:T(8,128)}) %all-reduce.5.cloned.1.call-update) | async-done | bytes 131088 | tf_op jit(solution)/shard_map/psum | solution.py:87
  121.9 0.9 fusion.71
  122.8 0.1 convert_element_type.120
  122.9 1.0 fusion.92
  123.9 2.7 copy-done.2
  126.6 0.8 multiply_reduce_fusion.1
  127.4 70.8 %all-gather.7.cloned.1.call-done = bf16[1,3072,768]{2,1,0:T(8,128)(2,1)} async-done(((bf16[1,192,768]{2,1,0:T(8,128)(2,1)}), bf16[1,3072,768]{2,1,0:T(8,128)(2,1)}) %all-gather.7.cloned.1.call-update) | async-done | bytes 4718608 | tf_op jit(solution)/shard_map/all_gather | solution.py:99
  198.1 8.0 %fusion.32 = bf16[512,64]{0,1:T(8,128)(2,1)S(1)} fusion(f32[512,3072]{1,0:T(8,128)} %copy-done.2, s32[]{:T(128)S(6)} %select_n.2, bf16[1,3072,768]{2,1,0:T(8,128)(2,1)} %all-gather.7.cloned.1.call-done, f32[3072]{0:T(1024)S(1)} %bitcast.116, f32[3072]{0:T(1024)S(1)} %bitcast.117, f32[512]{0:T(512)S(1)} %add_rsqrt_fusion.1, ...), kind=kOutput, calls=%fused_computation.37 | convolution fusion | flops 2474934272 | bytes 12775428 | tf_op jit(solution)/shard_map/dot_general | solution.py:44
  206.2 0.1 copy.12
  206.3 0.8 convert_element_type.124
  207.0 1.0 fusion.93
  208.1 2.7 copy-done.1
  210.7 0.8 multiply_reduce_fusion
  211.5 0.0 all-to-all-done
  211.5 7.9 %fusion.30 = bf16[512,64]{0,1:T(8,128)(2,1)S(1)} fusion(f32[512,3072]{1,0:T(8,128)} %copy-done.1, s32[]{:T(128)S(6)} %select_n.2, bf16[3072,768]{1,0:T(8,128)(2,1)} %bitcast.22, f32[3072]{0:T(1024)S(1)} %bitcast.114, f32[3072]{0:T(1024)S(1)} %bitcast.115, f32[512]{0:T(512)S(1)} %add_rsqrt_fusion, f32[512]{0:T(512)S(1)} %broadcast_multiply_fusion, ...), kind=kOutput, calls=%fused_computation.35 | convolution fusion | flops 2474934272 | bytes 12775428 | tf_op jit(solution)/shard_map/dot_general | solution.py:44
  219.4 0.1 copy.14
  219.6 0.8 convert_element_type.134
  220.3 7.9 %fusion.31 = bf16[512,64]{0,1:T(8,128)(2,1)S(1)} fusion(f32[512,3072]{1,0:T(8,128)} %copy-done.1, s32[]{:T(128)S(6)} %select_n.2, bf16[3072,768]{1,0:T(8,128)(2,1)} %bitcast.22, f32[3072]{0:T(1024)S(1)} %bitcast.113, f32[3072]{0:T(1024)S(1)} %bitcast.112, f32[512]{0:T(512)S(1)} %add_rsqrt_fusion, f32[512]{0:T(512)S(1)} %broadcast_multiply_fusion, ...), kind=kOutput, calls=%fused_computation.36 | convolution fusion | flops 2474934272 | bytes 12775428 | tf_op jit(solution)/shard_map/dot_general | solution.py:44
  228.3 0.1 copy.13
  228.4 0.7 convert_element_type.129
  229.1 0.0 all-reduce.9.cloned.1.call-update
  229.1 0.0 reduce-scatter.2.cloned.1.call-start
  229.2 40.5 %all-reduce.9.cloned.1.call-done = (bf16[256,128]{1,0:T(8,128)(2,1)}, bf16[256,128]{1,0:T(8,128)(2,1)}, bf16[256,128]{1,0:T(8,128)(2,1)}) async-done(((bf16[256,128]{1,0:T(8,128)(2,1)}, bf16[256,128]{1,0:T(8,128)(2,1)}, bf16[256,128]{1,0:T(8,128)(2,1)}), (bf16[256,128]{1,0:T(8,128)(2,1)}, bf16[256,128]{1,0:T(8,128)(2,1)}, bf16[256,128]{1,0:T(8,128)(2,1)})) %all-reduce.9.cloned.1.call-update) | async-done | bytes 196624 | tf_op jit(solution)/shard_map/psum | solution.py:119
  269.7 1.5 abs_reduce_fusion
  271.2 37.2 %psum.46 = f32[]{:T(128)} all-reduce(f32[]{:T(128)} %abs_reduce_fusion), channel_id=1, replica_groups=mesh['mp'=4,'fsdp'=16,'dp'=4] {'fsdp'}, use_global_device_ids=true, to_apply=%region_11.12 | all-reduce | flops 1 | bytes 8 | tf_op jit(solution)/shard_map/psum | solution.py:129
  309.1 1.6 multiply_convert_fusion
  310.7 0.1 reshape.203
  310.8 8.2 %convolution_convert_fusion = bf16[3072,768]{1,0:T(8,128)(2,1)} fusion(bf16[512,64]{1,0:T(8,128)(2,1)S(1)} %reshape.203, bf16[3,64,768]{2,1,0:T(8,128)(2,1)S(1)} %copy-done.8, f32[512,3072]{1,0:T(8,128)} %copy-done, f32[3072]{0:T(1024)S(1)} %bitcast.109, f32[3072]{0:T(1024)S(1)} %bitcast.111, f32[512]{0:T(512)S(1)} %add_rsqrt_fusion.2, ...), kind=kOutput, calls=%fused_computation.7 | convolution fusion | flops 2476867584 | bytes 11268096 | tf_op jit(solution)/shard_map/dot_general | solution.py:138
  319.0 0.0 reduce-scatter.2.cloned.1.call-update
  319.1 0.0 all-reduce.7.cloned.1.call-start
  319.1 82.7 %reduce-scatter.2.cloned.1.call-done = bf16[192,768]{1,0:T(8,128)(2,1)} async-done(((bf16[3072,768]{1,0:T(8,128)(2,1)}), bf16[192,768]{1,0:T(8,128)(2,1)}) %reduce-scatter.2.cloned.1.call-update) | async-done | bytes 294928 | tf_op jit(solution)/shard_map/reduce_scatter | solution.py:137
  401.8 0.0 all-reduce.7.cloned.1.call-update
  401.8 53.7 %all-reduce.7.cloned.1.call-done = bf16[192,768]{1,0:T(8,128)(2,1)} async-done(((bf16[192,768]{1,0:T(8,128)(2,1)}), bf16[192,768]{1,0:T(8,128)(2,1)}) %all-reduce.7.cloned.1.call-update) | async-done | bytes 294928 | tf_op jit(solution)/shard_map/psum | solution.py:145
  455.5 1.8 convert_element_type.139
  (39 shorter events, 0.5 us)
Async XLA Ops:
  7.2 34.4 %copy-start.5 = (bf16[3,64,3072]{2,1,0:T(8,128)(2,1)S(1)}, bf16[3,64,3072]{2,1,0:T(8,128)(2,1)}, u32[]{:S(2)}) copy-start(bf16[3,64,3072]{2,1,0:T(8,128)(2,1)} %param.14) | copy-start | bytes 3538948
  7.2 65.3 %all-gather.5.cloned.1.call-start = ((), (), s32[]{:S(2)}) async-start(), calls=%async_computation.5 | async-start | bytes 5013504 | tf_op jit(solution)/shard_map/all_gather | solution.py:84
  9.2 112.6 %all-reduce.5.cloned.1.call-start = ((), (), s32[]{:S(2)}) async-start(), calls=%async_computation.2 | async-start | bytes 262144 | tf_op jit(solution)/shard_map/psum | solution.py:87
  42.7 2.7 copy-start
  42.7 29.9 %copy-start.8 = (bf16[3,64,768]{2,1,0:T(8,128)(2,1)S(1)}, bf16[3,64,768]{2,1,0:T(8,128)(2,1)}, u32[]{:S(2)}) copy-start(bf16[3,64,768]{2,1,0:T(8,128)(2,1)} %param.17) | copy-start | bytes 884740
  72.5 9.4 %copy-start.3 = (bf16[3,192,768]{2,1,0:T(8,128)(2,1)S(1)}, bf16[3,192,768]{2,1,0:T(8,128)(2,1)}, u32[]{:S(2)}) copy-start(bf16[3,192,768]{2,1,0:T(8,128)(2,1)} %param.16) | copy-start | bytes 2654212
  81.1 117.0 %all-gather.7.cloned.1.call-start = ((), (), s32[]{:S(2)}) async-start(), calls=%async_computation.6 | async-start | bytes 5013504 | tf_op jit(solution)/shard_map/all_gather | solution.py:99
  82.4 2.1 copy-start.4
  84.5 37.4 %copy-start.6 = (f32[1,256,128]{2,1,0:T(8,128)S(1)}, f32[1,256,128]{2,1,0:T(8,128)}, u32[]{:S(2)}) copy-start(f32[1,256,128]{2,1,0:T(8,128)} %param.10) | copy-start | bytes 393220
  84.5 127.0 %all-to-all-start = ((bf16[16,192,768]{2,1,0:T(8,128)(2,1)}), bf16[16,192,768]{2,1,0:T(8,128)(2,1)}, u32[]{:S(2)}, u32[]{:S(2)}) async-start(bf16[16,192,768]{2,1,0:T(8,128)(2,1)} %bitcast.106), calls=%async_computation | async-start | bytes 9437184 | tf_op jit(solution)/shard_map/all_to_all | solution.py:17
  90.4 179.3 %all-reduce.9.cloned.1.call-start = ((), (), s32[]{:S(2)}) async-start(), calls=%async_computation.7 | async-start | bytes 393216 | tf_op jit(solution)/shard_map/psum | solution.py:119
  123.9 2.7 copy-start.2
  208.1 2.7 copy-start.1
  220.3 49.4 %copy-start.7 = (f32[256,128]{1,0:T(8,128)S(1)}, f32[256,128]{1,0:T(8,128)}, u32[]{:S(2)}) copy-start(f32[256,128]{1,0:T(8,128)} %all-reduce.5.cloned.1.call-done) | copy-start | bytes 393220
  229.1 172.7 %reduce-scatter.2.cloned.1.call-start = ((), (), s32[]{:S(2)}) async-start(), calls=%async_computation.3 | async-start | bytes 5013504 | tf_op jit(solution)/shard_map/reduce_scatter | solution.py:137
  319.1 136.5 %all-reduce.7.cloned.1.call-start = ((), (), s32[]{:S(2)}) async-start(), calls=%async_computation.4 | async-start | bytes 589824 | tf_op jit(solution)/shard_map/psum | solution.py:145
Sparse Core Ops, SparseCore 0:
  10.4 62.0 all-gather.4
  81.3 40.5 all-reduce.4
  125.2 72.9 all-gather.6
  229.3 40.3 all-reduce.8
  319.2 82.5 reduce-scatter.1
  404.3 51.1 all-reduce.6
